TPU v7x, 32 devices: a whole 2x2x4 slice. The times are simulated.
32 devices in a mesh: rows: 8 (over y, x, core), feat: 4 (over z).
Axes of the slice: x: 2, y: 2, z: 4, core: 2. Of those that a mesh axis runs over, the one named last changes fastest.
Arguments:
- queries: bfloat16 [49152, 4096], P('rows', 'feat'), may hold values from -6 to 6
- projection: bfloat16 [4096, 128], P('feat'), may hold values from -0.09375 to 0.09375
- models: float32 [64, 128], replicated, may hold values from -0.5 to 0.5
- first: int32 [49152], P('rows'), may hold values from 0 to 63
- second: int32 [49152], P('rows'), may hold values from 0 to 63
- wins: int32 [49152], P('rows'), may hold values 0 or 1
Outputs:
- update_proj: float32 [4096, 128], P('feat')
- update_models: float32 [64, 128], replicated
- loss: float32 [], replicated
All inputs are finite; a program needn't handle non-finite values. No bound on the sum of `wins` on one device may be relied on, other than what follows from the above.
Results may differ from a plain program's by a relative error of at most 0.00045.
The roundings to bfloat16 on the way count: a program that leaves them out, or rounds other values in their place, can miss the bound.
Values may be sent and summed in bfloat16 or wider, within the bound.
A program may use at most 64 MiB of HBM per device.

v0:
```python
import jax
import jax.numpy as jnp
from jax import lax
from jax.sharding import PartitionSpec as P

D = 4096
R = 128
NM = 64


def pair_gap(models, first, second):
    return jnp.take(models, first, axis=0) - jnp.take(models, second, axis=0)


def pick_table(models, first, second):
    labels = jnp.arange(models.shape[0], dtype=jnp.int32)[:, None]
    return (labels == first[None, :]).astype(jnp.float32) - (labels == second[None, :]).astype(
        jnp.float32
    )


def body(queries, projection, models, first, second, wins):
    local_rows = queries.shape[0]
    total_rows = float(local_rows * lax.axis_size("rows"))
    partial_value = jnp.dot(queries, projection, preferred_element_type=jnp.float32)
    gap = pair_gap(models, first, second)
    margin = lax.psum(jnp.sum(partial_value * gap, axis=-1), "feat")
    sign = 2.0 * wins.astype(jnp.float32) - 1.0
    loss_part = jnp.sum(jax.nn.softplus(-sign * margin)) / total_rows
    coef = -sign * jax.nn.sigmoid(-sign * margin) / total_rows
    back = (coef[:, None] * gap).astype(jnp.bfloat16)
    pick = pick_table(models, first, second)
    model_part = jnp.dot(pick, coef[:, None] * partial_value, precision=lax.Precision.HIGHEST)
    feat_count = float(lax.axis_size("feat"))
    grad_models, loss = lax.psum((model_part, loss_part / feat_count), ("rows", "feat"))
    model_square = jnp.sum(grad_models * grad_models)
    entries = jnp.sqrt(jnp.float32(D * R + NM * R))
    grad_local = jnp.dot(queries.T, back, preferred_element_type=jnp.float32)
    grad_proj = lax.psum(grad_local, "rows")
    square = lax.psum(jnp.sum(grad_proj * grad_proj), "feat")
    scale = entries / (jnp.sqrt(square + model_square) + 1e-06)
    update_proj = scale * grad_proj
    return (update_proj, scale * grad_models, loss)


def solution(mesh):
    in_specs = (P("rows", "feat"), P("feat", None), P(), P("rows"), P("rows"), P("rows"))
    out_specs = (P("feat", None), P(), P())
    return jax.shard_map(body, mesh=mesh, in_specs=in_specs, out_specs=out_specs, check_vma=False)
```

profile of v0, /device:TPU:0, one launch (start us, length us, event | category | flops | bytes accessed | tf_op | source)
XLA Modules:
  0.0 177.5 jit_solution(17190203566094224995)
XLA Ops:
  7.2 0.0 copy-start
  7.2 0.0 copy-start.1
  7.2 0.0 all-reduce.3.cloned.1.call-start
  7.2 0.7 fusion.14
  8.0 0.8 compare_and_fusion
  8.8 0.7 fusion.13
  9.5 0.0 copy-done.1
  9.5 20.9 %gather_fusion.1 = f32[6144,128]{1,0:T(8,128)} fusion(f32[64,128]{1,0:T(8,128)S(1)} %copy-done.1, s32[6144]{0:T(1024)S(1)} %fusion.14), kind=kCustom, calls=%fused_computation.1.clone | custom fusion | bytes 6316032 | tf_op jit(solution)/shard_map/jit(_take)/gather | solution.py:12
  30.4 2.4 %copy.10 = f32[6144,128]{0,1:T(8,128)S(1)} copy(f32[6144,128]{1,0:T(8,128)} %gather_fusion.1) | data formatting | bytes 6291456 | tf_op jit(solution)/shard_map/jit(_take)/gather | solution.py:12
  32.8 20.9 %gather_fusion = f32[6144,128]{1,0:T(8,128)} fusion(f32[64,128]{1,0:T(8,128)S(1)} %copy-done.1, s32[6144]{0:T(1024)S(1)} %fusion.13), kind=kCustom, calls=%fused_computation.clone | custom fusion | bytes 6316032 | tf_op jit(solution)/shard_map/jit(_take)/gather | solution.py:12
  53.7 3.5 %copy.9 = f32[6144,128]{0,1:T(8,128)} copy(f32[6144,128]{1,0:T(8,128)} %gather_fusion) | data formatting | bytes 6291456 | tf_op jit(solution)/shard_map/jit(_take)/gather | solution.py:12
  57.2 0.0 copy-done
  57.2 0.0 copy-start.4
  57.2 11.7 %multiply_reduce_fusion = (f32[6144]{0:T(1024)S(1)}, f32[6144,128]{0,1:T(8,128)}) fusion(f32[6144,128]{0,1:T(8,128)S(1)} %copy.10, pred[6144]{0:T(1024)(128)(4,1)S(1)} %get-tuple-element.13, f32[6144,128]{0,1:T(8,128)} %copy.9, pred[6144]{0:T(1024)(128)(4,1)S(1)} %get-tuple-element.14, bf16[6144,1024]{1,0:T(8,128)(2,1)} %param.8, ...), kind=kOutput, calls=%fused_computation.6 | convolution fusion | flops 1614538752 | bytes 22319104 | tf_op jit(solution)/shard_map/dot_general | solution.py:25
  68.9 20.8 %psum.35 = f32[6144]{0:T(1024)S(1)} all-reduce(f32[6144]{0:T(1024)S(1)} %get-tuple-element.11), channel_id=1, replica_groups=mesh['rows'=8,'feat'=4] {'feat'}, use_global_device_ids=true, to_apply=%region_1.3 | all-reduce | flops 6144 | bytes 49152 | tf_op jit(solution)/shard_map/psum | solution.py:27
  89.6 0.0 copy-done.4
  89.6 0.6 fusion.11
  90.3 0.0 copy-start.2
  90.3 0.0 copy-start.3
  90.3 8.3 %fusion.8 = f32[1024,128]{0,1:T(8,128)} fusion(bf16[6144,1024]{1,0:T(8,128)(2,1)} %param.8, f32[6144]{0:T(1024)S(1)} %get-tuple-element.10, f32[6144,128]{0,1:T(8,128)S(1)} %copy.10, f32[6144,128]{0,1:T(8,128)} %copy.9, pred[6144]{0:T(1024)(128)(4,1)S(1)} %get-tuple-element.13, pred[6144]{0:T(1024)(128)(4,1)S(1)} %get-tuple-element.14), kind=kOutput, calls=%fused_computation.15 | convolution fusion | flops 1614544896 | bytes 19435520 | tf_op jit(solution)/shard_map/dot_general | solution.py:38
  98.6 0.0 all-reduce.3.cloned.1.call-update
  99.2 0.0 copy-done.2
  99.2 0.0 copy-done.3
  99.3 5.2 %fusion = f32[64,128]{1,0:T(8,128)S(1)} fusion(f32[6144,128]{0,1:T(8,128)} %get-tuple-element.12, f32[6144]{0:T(1024)S(1)} %get-tuple-element.10, s32[6144]{0:T(1024)S(1)} %copy-done.2, s32[6144]{0:T(1024)S(1)} %copy-done.3), kind=kOutput, calls=%fused_computation.3 | convolution fusion | flops 606732288 | bytes 3252224 | tf_op jit(solution)/shard_map/dot_general | solution.py:33
  104.4 38.9 %all-reduce = (f32[64,128]{1,0:T(8,128)S(1)}, f32[]{:T(128)}) all-reduce(f32[64,128]{1,0:T(8,128)S(1)} %fusion, f32[]{:T(128)S(6)} %div.20), channel_id=1, replica_groups=mesh['rows'=8,'feat'=4] {'rows','feat'}, use_global_device_ids=true, to_apply=%region_5.7 | all-reduce | flops 8193 | bytes 65544 | tf_op jit(solution)/shard_map/psum | solution.py:35
  143.3 8.6 %all-reduce.3.cloned.1.call-done = f32[1024,128]{0,1:T(8,128)} async-done(((f32[1024,128]{0,1:T(8,128)}), f32[1024,128]{0,1:T(8,128)}) %all-reduce.3.cloned.1.call-update) | async-done | bytes 524304 | tf_op jit(solution)/shard_map/psum | solution.py:39
  151.9 1.8 %multiply_reduce_fusion.1 = f32[]{:T(128)} fusion(f32[1024,128]{0,1:T(8,128)} %all-reduce.3.cloned.1.call-done), kind=kLoop, calls=%fused_computation.18 | loop fusion | flops 262143 | bytes 524292 | tf_op jit(solution)/shard_map/reduce_sum | solution.py:40
  153.7 0.6 multiply_reduce_fusion.2
  154.3 12.2 %psum.37 = f32[]{:T(128)} all-reduce(f32[]{:T(128)} %multiply_reduce_fusion.1), channel_id=1, replica_groups=mesh['rows'=8,'feat'=4] {'feat'}, use_global_device_ids=true, to_apply=%region_4.6 | all-reduce | flops 1 | bytes 8 | tf_op jit(solution)/shard_map/psum | solution.py:40
  168.0 0.6 broadcast_multiply_fusion.1
  168.6 1.1 broadcast_multiply_fusion
  169.7 1.0 copy.11
Async XLA Ops:
  7.2 50.0 %copy-start = (bf16[1024,128]{1,0:T(8,128)(2,1)S(1)}, bf16[1024,128]{1,0:T(8,128)(2,1)}, u32[]{:S(2)}) copy-start(bf16[1024,128]{1,0:T(8,128)(2,1)} %param.9) | copy-start | bytes 786436
  7.2 2.3 %copy-start.1 = (f32[64,128]{1,0:T(8,128)S(1)}, f32[64,128]{1,0:T(8,128)}, u32[]{:S(2)}) copy-start(f32[64,128]{1,0:T(8,128)} %param.10) | copy-start | bytes 98308
  7.2 144.8 %all-reduce.3.cloned.1.call-start = ((), (), s32[]{:S(2)}) async-start(), calls=%async_computation | async-start | bytes 1048576 | tf_op jit(solution)/shard_map/psum | solution.py:39
  57.2 32.4 %copy-start.4 = (s32[6144]{0:T(1024)S(1)}, s32[6144]{0:T(1024)}, u32[]{:S(2)}) copy-start(s32[6144]{0:T(1024)} %param.13) | copy-start | bytes 73732
  90.3 9.0 %copy-start.2 = (s32[6144]{0:T(1024)S(1)}, s32[6144]{0:T(1024)}, u32[]{:S(2)}) copy-start(s32[6144]{0:T(1024)} %param.12) | copy-start | bytes 73732
  90.3 9.0 %copy-start.3 = (s32[6144]{0:T(1024)S(1)}, s32[6144]{0:T(1024)}, u32[]{:S(2)}) copy-start(s32[6144]{0:T(1024)} %param.11) | copy-start | bytes 73732
Sparse Core Ops, SparseCore 0:
  98.7 53.1 all-reduce.2
where the time goes:
time: 178 us
  blocking collectives  71.9 us (40%)
  local copies, waits for them, and re-layouts  48.7 us (27%)
  matrix products  25.1 us (14%)
  between operations  16.1 us (9%)
  waiting for transfers between devices  8.62 us (5%)
  other arithmetic  6.98 us (4%)
    gather x4, local copies, waits for them, and re-layouts, pair_gap(): return jnp.take(models, first, axis=0) - jnp.take(models, second, axis=0)  47.7 us
    psum x1, blocking collectives, body(): lax.psum((model_part, loss_part / feat_count), ('rows', 'feat'))  38.9 us
    psum x1, blocking collectives, body(): margin = lax.psum(jnp.sum(partial_value * gap, axis=-1), 'feat')  20.8 us
    psum x1, blocking collectives, body(): square = lax.psum(jnp.sum(grad_proj * grad_proj), 'feat')  12.2 us
    dot_general x1, matrix products, body(): jnp.dot(queries, projection, preferred_element_type=jnp.float32)  11.7 us
    psum x1, waiting for transfers between devices, body(): grad_proj = lax.psum(grad_local, 'rows')  8.61 us
    dot_general x1, matrix products, body(): grad_local = jnp.dot(queries.T, back, preferred_element_type=jnp.float32)  8.29 us
    dot_general x1, matrix products, body(): jnp.dot(pick, coef[:, None] * partial_value, precision=lax.Precision.HIGH...  5.18 us
  transfers between devices with their start and end apart: 1, of which 1 were waited for; matrix products, arithmetic and copies ran while one was open for 3% of the time, Pallas kernels for 0%

commit v1 on v0

--- a/solution.py
+++ b/solution.py
@@ -32,7 +32,7 @@
     pick = pick_table(models, first, second)
     model_part = jnp.dot(pick, coef[:, None] * partial_value, precision=lax.Precision.HIGHEST)
     feat_count = float(lax.axis_size("feat"))
-    grad_models, loss = lax.psum((model_part, loss_part / feat_count), ("rows", "feat"))
+    grad_models, loss = lax.psum(lax.psum((model_part, loss_part / feat_count), "rows"), "feat")
     model_square = jnp.sum(grad_models * grad_models)
     entries = jnp.sqrt(jnp.float32(D * R + NM * R))
     grad_local = jnp.dot(queries.T, back, preferred_element_type=jnp.float32)

time: 178 us -> 186 us (1.045)
  waiting for transfers between devices: 8.62 us -> 24.1 us
  blocking collectives: 71.9 us -> 64.4 us
    psum x1, blocking collectives: 38.9 us -> 23.4 us  [body(): lax.psum((model_part, loss_part / feat_count), 'rows')]
    psum x1, waiting for transfers between devices: 8.61 us -> 24.1 us  [body(): grad_proj = lax.psum(grad_local, 'rows')]
    psum x1, blocking collectives: 12.2 us -> 20.3 us  [body(): square = lax.psum(jnp.sum(grad_proj * grad_proj), 'feat')]
where the time goes in v1:
time: 186 us; the launch traced here: 185 us
  blocking collectives  64.4 us (35%)
  local copies, waits for them, and re-layouts  48.7 us (26%)
  matrix products  25.1 us (13%)
  waiting for transfers between devices  24.1 us (13%)
  between operations  16.1 us (9%)
  other arithmetic  6.98 us (4%)
    gather x4, local copies, waits for them, and re-layouts, pair_gap(): return jnp.take(models, first, axis=0) - jnp.take(models, second, axis=0)  47.7 us
    psum x1, waiting for transfers between devices, body(): grad_proj = lax.psum(grad_local, 'rows')  24.1 us
    psum x1, blocking collectives, body(): lax.psum((model_part, loss_part / feat_count), 'rows')  23.4 us
    psum x1, blocking collectives, body(): margin = lax.psum(jnp.sum(partial_value * gap, axis=-1), 'feat')  20.8 us
    psum x1, blocking collectives, body(): square = lax.psum(jnp.sum(grad_proj * grad_proj), 'feat')  20.3 us
    dot_general x1, matrix products, body(): jnp.dot(queries, projection, preferred_element_type=jnp.float32)  11.7 us
    dot_general x1, matrix products, body(): grad_local = jnp.dot(queries.T, back, preferred_element_type=jnp.float32)  8.29 us
    dot_general x1, matrix products, body(): jnp.dot(pick, coef[:, None] * partial_value, precision=lax.Precision.HIGH...  5.18 us
  transfers between devices with their start and end apart: 1, of which 1 were waited for; matrix products, arithmetic and copies ran while one was open for 3% of the time, Pallas kernels for 0%

profile of v1, /device:TPU:0, one launch (start us, length us, event | category | flops | bytes accessed | tf_op | source)
XLA Modules:
  0.0 185.4 jit_solution(5378575236596506585)
XLA Ops:
  7.2 0.0 copy-start
  7.2 0.0 copy-start.1
  7.2 0.0 all-reduce.4.cloned.1.call-start
  7.2 0.7 fusion.14
  8.0 0.8 compare_and_fusion
  8.8 0.7 fusion.13
  9.5 0.0 copy-done.1
  9.5 20.9 %gather_fusion.1 = f32[6144,128]{1,0:T(8,128)} fusion(f32[64,128]{1,0:T(8,128)S(1)} %copy-done.1, s32[6144]{0:T(1024)S(1)} %fusion.14), kind=kCustom, calls=%fused_computation.1.clone | custom fusion | bytes 6316032 | tf_op jit(solution)/shard_map/jit(_take)/gather | solution.py:12
  30.4 2.4 %copy.10 = f32[6144,128]{0,1:T(8,128)S(1)} copy(f32[6144,128]{1,0:T(8,128)} %gather_fusion.1) | data formatting | bytes 6291456 | tf_op jit(solution)/shard_map/jit(_take)/gather | solution.py:12
  32.8 20.9 %gather_fusion = f32[6144,128]{1,0:T(8,128)} fusion(f32[64,128]{1,0:T(8,128)S(1)} %copy-done.1, s32[6144]{0:T(1024)S(1)} %fusion.13), kind=kCustom, calls=%fused_computation.clone | custom fusion | bytes 6316032 | tf_op jit(solution)/shard_map/jit(_take)/gather | solution.py:12
  53.7 3.5 %copy.9 = f32[6144,128]{0,1:T(8,128)} copy(f32[6144,128]{1,0:T(8,128)} %gather_fusion) | data formatting | bytes 6291456 | tf_op jit(solution)/shard_map/jit(_take)/gather | solution.py:12
  57.2 0.0 copy-done
  57.2 0.0 copy-start.4
  57.2 11.7 %multiply_reduce_fusion = (f32[6144]{0:T(1024)S(1)}, f32[6144,128]{0,1:T(8,128)}) fusion(f32[6144,128]{0,1:T(8,128)S(1)} %copy.10, pred[6144]{0:T(1024)(128)(4,1)S(1)} %get-tuple-element.16, f32[6144,128]{0,1:T(8,128)} %copy.9, pred[6144]{0:T(1024)(128)(4,1)S(1)} %get-tuple-element.17, bf16[6144,1024]{1,0:T(8,128)(2,1)} %param.8, ...), kind=kOutput, calls=%fused_computation.6 | convolution fusion | flops 1614538752 | bytes 22319104 | tf_op jit(solution)/shard_map/dot_general | solution.py:25
  68.9 20.8 %psum.49 = f32[6144]{0:T(1024)S(1)} all-reduce(f32[6144]{0:T(1024)S(1)} %get-tuple-element.14), channel_id=1, replica_groups=mesh['rows'=8,'feat'=4] {'feat'}, use_global_device_ids=true, to_apply=%region_1.3 | all-reduce | flops 6144 | bytes 49152 | tf_op jit(solution)/shard_map/psum | solution.py:27
  89.6 0.0 copy-done.4
  89.6 0.6 fusion.11
  90.3 0.0 copy-start.2
  90.3 0.0 copy-start.3
  90.3 8.3 %fusion.8 = f32[1024,128]{0,1:T(8,128)} fusion(bf16[6144,1024]{1,0:T(8,128)(2,1)} %param.8, f32[6144]{0:T(1024)S(1)} %get-tuple-element.13, f32[6144,128]{0,1:T(8,128)S(1)} %copy.10, f32[6144,128]{0,1:T(8,128)} %copy.9, pred[6144]{0:T(1024)(128)(4,1)S(1)} %get-tuple-element.16, pred[6144]{0:T(1024)(128)(4,1)S(1)} %get-tuple-element.17), kind=kOutput, calls=%fused_computation.15 | convolution fusion | flops 1614544896 | bytes 19435520 | tf_op jit(solution)/shard_map/dot_general | solution.py:38
  98.6 0.0 all-reduce.4.cloned.1.call-update
  99.2 0.0 copy-done.2
  99.2 0.0 copy-done.3
  99.3 5.2 %fusion = f32[64,128]{1,0:T(8,128)S(1)} fusion(f32[6144,128]{0,1:T(8,128)} %get-tuple-element.15, f32[6144]{0:T(1024)S(1)} %get-tuple-element.13, s32[6144]{0:T(1024)S(1)} %copy-done.2, s32[6144]{0:T(1024)S(1)} %copy-done.3), kind=kOutput, calls=%fused_computation.3 | convolution fusion | flops 606732288 | bytes 3252224 | tf_op jit(solution)/shard_map/dot_general | solution.py:33
  104.4 23.4 %all-reduce = (f32[64,128]{1,0:T(8,128)S(1)}, f32[]{:T(128)}) all-reduce(f32[64,128]{1,0:T(8,128)S(1)} %fusion, f32[]{:T(128)S(6)} %div.20), channel_id=1, replica_groups=mesh['rows'=8,'feat'=4] {'rows'}, use_global_device_ids=true, to_apply=%region_5.7 | all-reduce | flops 8193 | bytes 65544 | tf_op jit(solution)/shard_map/psum | solution.py:35
  127.8 24.1 %all-reduce.4.cloned.1.call-done = f32[1024,128]{0,1:T(8,128)} async-done(((f32[1024,128]{0,1:T(8,128)}), f32[1024,128]{0,1:T(8,128)}) %all-reduce.4.cloned.1.call-update) | async-done | bytes 524304 | tf_op jit(solution)/shard_map/psum | solution.py:39
  151.9 1.8 multiply_reduce_fusion.1
  153.7 20.3 %all-reduce.1 = (f32[]{:T(128)}, f32[64,128]{1,0:T(8,128)S(1)}, f32[]{:T(128)}) all-reduce(f32[]{:T(128)} %multiply_reduce_fusion.1, f32[64,128]{1,0:T(8,128)S(1)} %get-tuple-element.7, f32[]{:T(128)} %get-tuple-element.8), channel_id=1, replica_groups=mesh['rows'=8,'feat'=4] {'feat'}, use_global_device_ids=true, to_apply=%region_4.6 | all-reduce | flops 8194 | bytes 65552 | tf_op jit(solution)/shard_map/psum | solution.py:40
  173.9 0.6 multiply_reduce_fusion.2
  175.9 0.6 broadcast_multiply_fusion.1
  176.5 1.1 broadcast_multiply_fusion
  177.6 1.0 copy.11
Async XLA Ops:
  7.2 50.0 %copy-start = (bf16[1024,128]{1,0:T(8,128)(2,1)S(1)}, bf16[1024,128]{1,0:T(8,128)(2,1)}, u32[]{:S(2)}) copy-start(bf16[1024,128]{1,0:T(8,128)(2,1)} %param.9) | copy-start | bytes 786436
  7.2 2.3 %copy-start.1 = (f32[64,128]{1,0:T(8,128)S(1)}, f32[64,128]{1,0:T(8,128)}, u32[]{:S(2)}) copy-start(f32[64,128]{1,0:T(8,128)} %param.10) | copy-start | bytes 98308
  7.2 144.7 %all-reduce.4.cloned.1.call-start = ((), (), s32[]{:S(2)}) async-start(), calls=%async_computation | async-start | bytes 1048576 | tf_op jit(solution)/shard_map/psum | solution.py:39
  57.2 32.4 %copy-start.4 = (s32[6144]{0:T(1024)S(1)}, s32[6144]{0:T(1024)}, u32[]{:S(2)}) copy-start(s32[6144]{0:T(1024)} %param.13) | copy-start | bytes 73732
  90.3 9.0 %copy-start.2 = (s32[6144]{0:T(1024)S(1)}, s32[6144]{0:T(1024)}, u32[]{:S(2)}) copy-start(s32[6144]{0:T(1024)} %param.12) | copy-start | bytes 73732
  90.3 9.0 %copy-start.3 = (s32[6144]{0:T(1024)S(1)}, s32[6144]{0:T(1024)}, u32[]{:S(2)}) copy-start(s32[6144]{0:T(1024)} %param.11) | copy-start | bytes 73732
Sparse Core Ops, SparseCore 0:
  98.7 53.1 all-reduce.3
